TPU v7x, 128 devices: a whole 4x4x4 slice. The times are simulated.
128 devices in a mesh: replica: 32 (over y, x, z_lo), tensor: 4 (over z_hi, core).
Axes of the slice: x: 4, y: 4, z: 4 (z_hi: 2, z_lo: 2; z = z_hi * 2 + z_lo), core: 2. Of those that a mesh axis runs over, the one named last changes fastest.
Arguments:
- weight: bfloat16 [32, 4096, 2048], P('replica', None, 'tensor'), may hold values from -0.09375 to 0.09375
- momentum: bfloat16 [32, 4096, 2048], P('replica', None, 'tensor'), may hold values from -24 to 24
- inputs: bfloat16 [2, 16384, 4096], P(None, ('replica', 'tensor')), may hold values from -6 to 6
- out_grads: bfloat16 [2, 16384, 2048], P(None, 'replica', 'tensor'), may hold values from -6 to 6
Outputs:
- new_weight: bfloat16 [32, 4096, 2048], P('replica', None, 'tensor')
- new_momentum: bfloat16 [32, 4096, 2048], P('replica', None, 'tensor')
- input_grad: bfloat16 [2, 16384, 4096], P(None, ('replica', 'tensor'))
All inputs are finite; a program needn't handle non-finite values.
Results may differ from a plain program's by a relative error of at most 0.014.
Values may be sent and summed in bfloat16 or wider, within the bound.
A program may use at most 128 MiB of HBM per device.

v0:
```python
import jax
import jax.numpy as jnp
from jax import lax
from jax.sharding import PartitionSpec as P

learn_rate = 0.001
mom_decay = 0.9


def in_blocks(shard, dim, devices):
    dims = shard.shape
    blocks = shard.reshape(*dims[:dim], devices, dims[dim] // devices, *dims[dim + 1 :])
    return jnp.moveaxis(blocks, dim, 0)


def sum_at_owner(shard, axis, dim):
    blocks = in_blocks(shard, dim, lax.axis_size(axis))
    arrived = lax.all_to_all(blocks, axis, split_axis=0, concat_axis=0, tiled=True)
    return arrived.astype(jnp.float32).sum(axis=0)


def from_partner(block, axis, distance):
    count = lax.axis_size(axis)
    route = []
    for low in range(count):
        high = low | 1 << distance
        if high != low and high < count:
            route += [(low, high), (high, low)]
    return lax.ppermute(block, axis, route)


def silu_slope(pre):
    sigma = jax.nn.sigmoid(pre)
    return sigma * (1.0 + pre * (1.0 - sigma))


def input_partials(slope_grad, weight_now):
    partial_value = lax.dot_general(
        slope_grad, weight_now, (((1,), (1,)), ((), ())), preferred_element_type=jnp.float32
    )
    rounded = partial_value.astype(jnp.bfloat16)
    return sum_at_owner(rounded, "tensor", 0).astype(jnp.bfloat16)


def gossip_update(weight_now, moment_now, grad_w, step):
    moment_new = (mom_decay * moment_now.astype(jnp.float32) + grad_w).astype(jnp.bfloat16)
    stepped = (weight_now.astype(jnp.float32) - learn_rate * moment_new.astype(jnp.float32)).astype(
        jnp.bfloat16
    )
    other_weight, other_moment = from_partner((stepped, moment_new), "replica", step)
    averaged = ((stepped.astype(jnp.float32) + other_weight.astype(jnp.float32)) * 0.5).astype(
        jnp.bfloat16
    )
    moment_avg = ((moment_new.astype(jnp.float32) + other_moment.astype(jnp.float32)) * 0.5).astype(
        jnp.bfloat16
    )
    return (averaged, moment_avg)


def local(weight, momentum, inputs, out_grads):
    weight_now = weight[0]
    moment_now = momentum[0]
    grads_out = []
    for step in range(inputs.shape[0]):
        rows_here = inputs[step]
        gathered = lax.all_gather(rows_here, "tensor", axis=0, tiled=True)
        pre = jnp.dot(gathered, weight_now, preferred_element_type=jnp.float32)
        slope_grad = (out_grads[step].astype(jnp.float32) * silu_slope(pre)).astype(jnp.bfloat16)
        grad_w = lax.dot_general(
            gathered, slope_grad, (((0,), (0,)), ((), ())), preferred_element_type=jnp.float32
        )
        grads_out.append(input_partials(slope_grad, weight_now))
        next_weight, next_moment = gossip_update(weight_now, moment_now, grad_w, step)
        weight_now = next_weight
        moment_now = next_moment
    return (weight_now[None], moment_now[None], jnp.stack(grads_out))


def solution(mesh):
    return jax.shard_map(
        local,
        mesh=mesh,
        in_specs=(
            P("replica", None, "tensor"),
            P("replica", None, "tensor"),
            P(None, ("replica", "tensor"), None),
            P(None, "replica", "tensor"),
        ),
        out_specs=(
            P("replica", None, "tensor"),
            P("replica", None, "tensor"),
            P(None, ("replica", "tensor"), None),
        ),
        check_vma=False,
    )
```

profile of v0, /device:TPU:0, one launch (start us, length us, event | category | flops | bytes accessed | tf_op | source)
XLA Modules:
  0.0 492.5 jit_solution(18293548097176699641)
XLA Ops:
  7.2 0.0 all-gather.5.cloned.1.call-start
  7.2 3.2 fusion.48
  10.4 0.0 all-gather.5.cloned.1.call-update
  10.4 0.0 all-gather.7.cloned.1.call-start
  10.4 0.7 all-gather.7.cloned.1.call-update
  11.1 6.3 %copy.8 = bf16[1,4096,512]{1,2,0:T(8,128)(2,1)} copy(bf16[1,4096,512]{2,1,0:T(8,128)(2,1)} %param.5) | data formatting | bytes 8388608 | tf_op args[1]
  17.5 6.4 %copy.7 = bf16[1,4096,512]{1,2,0:T(8,128)(2,1)} copy(bf16[1,4096,512]{2,1,0:T(8,128)(2,1)} %param.4) | data formatting | bytes 8388608 | tf_op args[0]
  23.8 0.0 copy-start.5
  23.9 27.8 %all-gather.5.cloned.1.call-done = bf16[1,512,4096]{2,1,0:T(8,128)(2,1)} async-done(((bf16[1,128,4096]{2,1,0:T(8,128)(2,1)}), bf16[1,512,4096]{2,1,0:T(8,128)(2,1)}) %all-gather.5.cloned.1.call-update) | async-done | bytes 4194320 | tf_op jit(solution)/shard_map/all_gather | solution.py:66
  51.7 0.0 copy-start.1
  51.7 0.0 copy-start.2
  51.7 0.0 copy-start.4
  51.7 5.9 %fusion.13 = f32[512,512]{1,0:T(8,128)S(1)} fusion(bf16[1,4096,512]{2,1,0:T(8,128)(2,1)} %param.4, bf16[1,512,4096]{2,1,0:T(8,128)(2,1)} %all-gather.5.cloned.1.call-done), kind=kOutput, calls=%fused_computation.23 | convolution fusion | flops 2147483648 | bytes 9437184 | tf_op jit(solution)/shard_map/dot_general | solution.py:67
  57.6 0.0 copy-done.5
  57.6 0.0 copy-done.1
  57.6 0.0 copy-done.2
  57.6 1.2 copy-done.4
  58.8 6.5 %fusion.1 = (bf16[4096,512]{0,1:T(8,128)(2,1)}, bf16[4096,512]{0,1:T(8,128)(2,1)}) fusion(bf16[1,4096,512]{1,2,0:T(8,128)(2,1)S(1)} %copy-done.2, bf16[1,512,4096]{2,1,0:T(8,128)(2,1)S(1)} %copy-done.4, f32[512,512]{1,0:T(8,128)S(1)} %fusion.13, bf16[2,512,512]{2,1,0:T(8,128)(2,1)S(1)} %copy-done.5, bf16[1,4096,512]{1,2,0:T(8,128)(2,1)S(1)} %copy-done.1), kind=kOutput, calls=%fused_computation.5 | convolution fusion | flops 2168979456 | bytes 22544384 | tf_op jit(solution)/shard_map/dot_general | solution.py:69
  65.3 0.5 collective-permute-start
  65.8 1.5 collective-permute-start.1
  67.4 46.2 %all-gather.7.cloned.1.call-done = bf16[1,512,4096]{2,1,0:T(8,128)(2,1)} async-done(((bf16[1,128,4096]{2,1,0:T(8,128)(2,1)}), bf16[1,512,4096]{2,1,0:T(8,128)(2,1)}) %all-gather.7.cloned.1.call-update) | async-done | bytes 4194320 | tf_op jit(solution)/shard_map/all_gather | solution.py:66
  113.5 0.0 copy-start.3
  113.5 65.3 %collective-permute-done = bf16[4096,512]{0,1:T(8,128)(2,1)} collective-permute-done((bf16[4096,512]{0,1:T(8,128)(2,1)}, bf16[4096,512]{0,1:T(8,128)(2,1)}, u32[]{:S(2)}, u32[]{:S(2)}) %collective-permute-start) | collective-permute-done | bytes 4194336 | tf_op jit(solution)/shard_map/ppermute | solution.py:29
  178.8 7.0 %fusion.23 = f32[512,512]{1,0:T(8,128)S(1)} fusion(bf16[1,512,4096]{2,1,0:T(8,128)(2,1)} %all-gather.7.cloned.1.call-done, bf16[4096,512]{0,1:T(8,128)(2,1)} %collective-permute-done, bf16[4096,512]{0,1:T(8,128)(2,1)} %get-tuple-element.10), kind=kOutput, calls=%fused_computation.32 | convolution fusion | flops 2157969408 | bytes 13631488 | tf_op jit(solution)/shard_map/dot_general | solution.py:67
  185.9 0.0 copy-start
  185.9 82.6 %collective-permute-done.1 = bf16[4096,512]{0,1:T(8,128)(2,1)} collective-permute-done((bf16[4096,512]{0,1:T(8,128)(2,1)}, bf16[4096,512]{0,1:T(8,128)(2,1)}, u32[]{:S(2)}, u32[]{:S(2)}) %collective-permute-start.1) | collective-permute-done | bytes 4194336 | tf_op jit(solution)/shard_map/ppermute | solution.py:29
  268.5 0.0 copy-done.3
  268.5 9.2 %fusion.8 = bf16[4096,512]{0,1:T(8,128)(2,1)} fusion(bf16[4096,512]{0,1:T(8,128)(2,1)} %collective-permute-done.1, bf16[4096,512]{0,1:T(8,128)(2,1)} %get-tuple-element.11, bf16[1,512,4096]{2,1,0:T(8,128)(2,1)S(1)} %copy-done.3, f32[512,512]{1,0:T(8,128)S(1)} %fusion.23, bf16[2,512,512]{2,1,0:T(8,128)(2,1)S(1)} %copy-done.5), kind=kOutput, calls=%fused_computation.13 | convolution fusion | flops 2168979456 | bytes 18350080 | tf_op jit(solution)/shard_map/dot_general | solution.py:69
  277.7 1.5 collective-permute-start.3
  279.2 0.0 copy-done
  279.2 4.5 convolution_convert_fusion.1
  283.7 4.9 all-to-all-start
  288.6 81.8 %collective-permute-done.3 = bf16[4096,512]{0,1:T(8,128)(2,1)} collective-permute-done((bf16[4096,512]{0,1:T(8,128)(2,1)}, bf16[4096,512]{0,1:T(8,128)(2,1)}, u32[]{:S(2)}, u32[]{:S(2)}) %collective-permute-start.3) | collective-permute-done | bytes 4194336 | tf_op jit(solution)/shard_map/ppermute | solution.py:29
  370.4 9.9 %fusion.11 = (bf16[1,4096,512]{1,2,0:T(8,128)(2,1)}, bf16[4096,512]{0,1:T(8,128)(2,1)}) fusion(bf16[4096,512]{0,1:T(8,128)(2,1)} %collective-permute-done.3, bf16[4096,512]{0,1:T(8,128)(2,1)} %fusion.8, bf16[4096,512]{0,1:T(8,128)(2,1)} %collective-permute-done, bf16[4096,512]{0,1:T(8,128)(2,1)} %get-tuple-element.10), kind=kLoop, calls=%fused_computation.21 | loop fusion | flops 29360128 | bytes 25165824 | tf_op jit(solution)/shard_map/broadcast_in_dim | solution.py:76
  380.2 1.5 collective-permute-start.2
  381.7 8.2 %convolution_convert_fusion = bf16[512,4096]{1,0:T(8,128)(2,1)} fusion(f32[512,512]{1,0:T(8,128)S(1)} %fusion.23, bf16[2,512,512]{2,1,0:T(8,128)(2,1)S(1)} %copy-done.5, bf16[4096,512]{0,1:T(8,128)(2,1)} %collective-permute-done, bf16[4096,512]{0,1:T(8,128)(2,1)} %get-tuple-element.10), kind=kOutput, calls=%fused_computation.18 | convolution fusion | flops 2162688000 | bytes 14155776 | tf_op jit(solution)/shard_map/dot_general | solution.py:38
  389.9 0.0 all-to-all-done
  389.9 4.9 all-to-all-start.1
  394.8 3.1 reduce_sum.24
  397.8 46.7 %all-to-all-done.1 = bf16[4,128,4096]{2,1,0:T(8,128)(2,1)} async-done(((bf16[4,128,4096]{2,1,0:T(8,128)(2,1)}), bf16[4,128,4096]{2,1,0:T(8,128)(2,1)}, u32[]{:S(2)}, u32[]{:S(2)}) %all-to-all-start.1) | async-done | bytes 4194336 | tf_op jit(solution)/shard_map/all_to_all | solution.py:18
  444.5 3.1 reduce_sum.25
  447.6 1.5 pad_maximum_fusion
  449.1 6.4 %copy.11 = bf16[1,4096,512]{2,1,0:T(8,128)(2,1)} copy(bf16[1,4096,512]{1,2,0:T(8,128)(2,1)} %get-tuple-element.6) | data formatting | bytes 8388608
  455.5 16.6 %collective-permute-done.2 = bf16[4096,512]{0,1:T(8,128)(2,1)} collective-permute-done((bf16[4096,512]{0,1:T(8,128)(2,1)}, bf16[4096,512]{0,1:T(8,128)(2,1)}, u32[]{:S(2)}, u32[]{:S(2)}) %collective-permute-start.2) | collective-permute-done | bytes 4194336 | tf_op jit(solution)/shard_map/ppermute | solution.py:29
  472.0 7.2 %fusion.10 = bf16[1,4096,512]{1,2,0:T(8,128)(2,1)} fusion(bf16[4096,512]{0,1:T(8,128)(2,1)} %collective-permute-done.2, bf16[4096,512]{0,1:T(8,128)(2,1)} %get-tuple-element.7), kind=kLoop, calls=%fused_computation.20 | loop fusion | flops 10485760 | bytes 12582912 | tf_op jit(solution)/shard_map/broadcast_in_dim | solution.py:76
  479.2 6.4 %copy.10 = bf16[1,4096,512]{2,1,0:T(8,128)(2,1)} copy(bf16[1,4096,512]{1,2,0:T(8,128)(2,1)} %fusion.10) | data formatting | bytes 8388608
Async XLA Ops:
  7.2 44.5 %all-gather.5.cloned.1.call-start = ((), (), s32[]{:S(2)}) async-start(), calls=%async_computation.2 | async-start | bytes 5242880 | tf_op jit(solution)/shard_map/all_gather | solution.py:66
  10.4 103.1 %all-gather.7.cloned.1.call-start = ((), (), s32[]{:S(2)}) async-start(), calls=%async_computation.3 | async-start | bytes 5242880 | tf_op jit(solution)/shard_map/all_gather | solution.py:66
  23.8 33.8 %copy-start.5 = (bf16[2,512,512]{2,1,0:T(8,128)(2,1)S(1)}, bf16[2,512,512]{2,1,0:T(8,128)(2,1)}, u32[]{:S(2)}) copy-start(bf16[2,512,512]{2,1,0:T(8,128)(2,1)} %param.7) | copy-start | bytes 3145732
  51.7 5.9 %copy-start.1 = (bf16[1,4096,512]{1,2,0:T(8,128)(2,1)S(1)}, bf16[1,4096,512]{1,2,0:T(8,128)(2,1)}, u32[]{:S(2)}) copy-start(bf16[1,4096,512]{1,2,0:T(8,128)(2,1)} %copy.8) | copy-start | bytes 12582916
  51.7 5.9 %copy-start.2 = (bf16[1,4096,512]{1,2,0:T(8,128)(2,1)S(1)}, bf16[1,4096,512]{1,2,0:T(8,128)(2,1)}, u32[]{:S(2)}) copy-start(bf16[1,4096,512]{1,2,0:T(8,128)(2,1)} %copy.7) | copy-start | bytes 12582916
  51.7 7.1 %copy-start.4 = (bf16[1,512,4096]{2,1,0:T(8,128)(2,1)S(1)}, bf16[1,512,4096]{2,1,0:T(8,128)(2,1)}, u32[]{:S(2)}) copy-start(bf16[1,512,4096]{2,1,0:T(8,128)(2,1)} %all-gather.5.cloned.1.call-done) | copy-start | bytes 12582916
  65.3 113.5 %collective-permute-start = (bf16[4096,512]{0,1:T(8,128)(2,1)}, bf16[4096,512]{0,1:T(8,128)(2,1)}, u32[]{:S(2)}, u32[]{:S(2)}) collective-permute-start(bf16[4096,512]{0,1:T(8,128)(2,1)} %get-tuple-element.10), channel_id=1, source_target_pairs={{0,4},{4,0},{8,12},{12,8},{16,20},{20,16},{24,28},{28,24},{32,36},... | collective-permute-start | bytes 12582920 | tf_op jit(solution)/shard_map/ppermute | solution.py:29
  65.8 202.6 %collective-permute-start.1 = (bf16[4096,512]{0,1:T(8,128)(2,1)}, bf16[4096,512]{0,1:T(8,128)(2,1)}, u32[]{:S(2)}, u32[]{:S(2)}) collective-permute-start(bf16[4096,512]{0,1:T(8,128)(2,1)} %get-tuple-element.11), channel_id=1, source_target_pairs={{0,4},{4,0},{8,12},{12,8},{16,20},{20,16},{24,28},{28,24},{32,36},... | collective-permute-start | bytes 12582920 | tf_op jit(solution)/shard_map/ppermute | solution.py:29
  113.5 155.0 %copy-start.3 = (bf16[1,512,4096]{2,1,0:T(8,128)(2,1)S(1)}, bf16[1,512,4096]{2,1,0:T(8,128)(2,1)}, u32[]{:S(2)}) copy-start(bf16[1,512,4096]{2,1,0:T(8,128)(2,1)} %all-gather.7.cloned.1.call-done) | copy-start | bytes 12582916
  185.9 93.3 %copy-start = (bf16[1,4096,512]{2,1,0:T(8,128)(2,1)S(1)}, bf16[1,4096,512]{2,1,0:T(8,128)(2,1)}, u32[]{:S(2)}) copy-start(bf16[1,4096,512]{2,1,0:T(8,128)(2,1)} %param.4) | copy-start | bytes 12582916
  277.7 92.7 %collective-permute-start.3 = (bf16[4096,512]{0,1:T(8,128)(2,1)}, bf16[4096,512]{0,1:T(8,128)(2,1)}, u32[]{:S(2)}, u32[]{:S(2)}) collective-permute-start(bf16[4096,512]{0,1:T(8,128)(2,1)} %fusion.8), channel_id=1, source_target_pairs={{0,8},{8,0},{4,12},{12,4},{16,24},{24,16},{20,28},{28,20},{32,40},... | collective-permute-start | bytes 12582920 | tf_op jit(solution)/shard_map/ppermute | solution.py:29
  283.7 106.2 %all-to-all-start = ((bf16[4,128,4096]{2,1,0:T(8,128)(2,1)}), bf16[4,128,4096]{2,1,0:T(8,128)(2,1)}, u32[]{:S(2)}, u32[]{:S(2)}) async-start(bf16[4,128,4096]{2,1,0:T(8,128)(2,1)} %bitcast.66), calls=%async_computation | async-start | bytes 8388608 | tf_op jit(solution)/shard_map/all_to_all | solution.py:18
  380.2 91.8 %collective-permute-start.2 = (bf16[4096,512]{0,1:T(8,128)(2,1)}, bf16[4096,512]{0,1:T(8,128)(2,1)}, u32[]{:S(2)}, u32[]{:S(2)}) collective-permute-start(bf16[4096,512]{0,1:T(8,128)(2,1)} %get-tuple-element.7), channel_id=1, source_target_pairs={{0,8},{8,0},{4,12},{12,4},{16,24},{24,16},{20,28},{28,20},{32,40},... | collective-permute-start | bytes 12582920 | tf_op jit(solution)/shard_map/ppermute | solution.py:29
  389.9 54.6 %all-to-all-start.1 = ((bf16[4,128,4096]{2,1,0:T(8,128)(2,1)}), bf16[4,128,4096]{2,1,0:T(8,128)(2,1)}, u32[]{:S(2)}, u32[]{:S(2)}) async-start(bf16[4,128,4096]{2,1,0:T(8,128)(2,1)} %bitcast.67), calls=%async_computation.1 | async-start | bytes 8388608 | tf_op jit(solution)/shard_map/all_to_all | solution.py:18
Sparse Core Ops, SparseCore 0:
  10.5 41.1 all-gather.4
  53.9 59.5 all-gather.6
where the time goes:
time: 493 us; the launch traced here: 492 us
  waiting for transfers between devices  368 us (75%)
  matrix products  41.4 us (8%)
  local copies, waits for them, and re-layouts  29.8 us (6%)
  other arithmetic  24.7 us (5%)
  starting transfers between devices  14.8 us (3%)
  between operations  14.1 us (3%)
    ppermute x4, waiting for transfers between devices, from_partner(): return lax.ppermute(block, axis, route)  246 us
    all_gather x2, waiting for transfers between devices, local(): gathered = lax.all_gather(rows_here, 'tensor', axis=0, tiled=True)  74 us
    all_to_all x2, waiting for transfers between devices, sum_at_owner(): lax.all_to_all(blocks, axis, split_axis=0, concat_axis=0, tiled=True)  46.7 us
    unnamed x16, local copies, waits for them, and re-layouts  26.7 us
    broadcast_in_dim x2, other arithmetic, local(): return (weight_now[None], moment_now[None], jnp.stack(grads_out))  17 us
    dot_general x2, matrix products, local(): lax.dot_general(gathered, slope_grad, (((0,), (0,)), ((), ())), preferred...  15.7 us
    dot_general x2, matrix products, local(): pre = jnp.dot(gathered, weight_now, preferred_element_type=jnp.float32)  13 us
    dot_general x2, matrix products, input_partials(): lax.dot_general(slope_grad, weight_now, (((1,), (1,)), ((), ())), preferr...  12.7 us
  transfers between devices with their start and end apart: 8, of which 7 were waited for; matrix products, arithmetic and copies ran while one was open for 14% of the time, Pallas kernels for 0%

commit v1 on v0

--- a/solution.py
+++ b/solution.py
@@ -63,7 +63,9 @@
     grads_out = []
     for step in range(inputs.shape[0]):
         rows_here = inputs[step]
-        gathered = lax.all_gather(rows_here, "tensor", axis=0, tiled=True)
+        gathered = jnp.concatenate(
+            lax.all_to_all(jnp.stack([rows_here] * lax.axis_size("tensor")), "tensor", 0, 0), axis=0
+        )
         pre = jnp.dot(gathered, weight_now, preferred_element_type=jnp.float32)
         slope_grad = (out_grads[step].astype(jnp.float32) * silu_slope(pre)).astype(jnp.bfloat16)
         grad_w = lax.dot_general(

time: 493 us -> 519 us (1.053)
  blocking collectives: 0 us -> 225 us
  waiting for transfers between devices: 368 us -> 184 us
  between operations: 14.1 us -> 0.78 us
  matrix products: 41.4 us -> 32.3 us
  starting transfers between devices: 14.8 us -> 20 us
    all_to_all x0 -> x1, blocking collectives: none -> 225 us  [local(): lax.all_to_all(jnp.stack([rows_here] * lax.axis_size('tensor')), 'tensor'...]
    ppermute x4, waiting for transfers between devices: 246 us -> 101 us  [from_partner(): return lax.ppermute(block, axis, route)]
    all_gather x2 -> x0, waiting for transfers between devices: 74 us -> none  [local(): gathered = lax.all_gather(rows_here, 'tensor', axis=0, tiled=True)]
    all_to_all x0 -> x1, waiting for transfers between devices: none -> 37 us  [local(): lax.all_to_all(jnp.stack([rows_here] * lax.axis_size('tensor')), 'tensor'...]
    all_to_all x0 -> x1, starting transfers between devices: none -> 5.23 us  [local(): lax.all_to_all(jnp.stack([rows_here] * lax.axis_size('tensor')), 'tensor'...]
    unnamed x16 -> x20, local copies, waits for them, and re-layouts: 26.7 us -> 25.8 us
  transfers between devices with their start and end apart: 8 -> 7, of which waited for: 7 -> 4; matrix products, arithmetic and copies ran while one was open for 14% -> 9% of each run, Pallas kernels for 0% -> 0%
where the time goes in v1:
time: 519 us; the launch traced here: 518 us
  blocking collectives  225 us (43%)
  waiting for transfers between devices  184 us (35%)
  matrix products  32.3 us (6%)
  local copies, waits for them, and re-layouts  30.6 us (6%)
  other arithmetic  24.6 us (5%)
  starting transfers between devices  20 us (4%)
    all_to_all x1, blocking collectives, local(): lax.all_to_all(jnp.stack([rows_here] * lax.axis_size('tensor')), 'tensor'...  225 us
    ppermute x4, waiting for transfers between devices, from_partner(): return lax.ppermute(block, axis, route)  101 us
    all_to_all x2, waiting for transfers between devices, sum_at_owner(): lax.all_to_all(blocks, axis, split_axis=0, concat_axis=0, tiled=True)  46.7 us
    all_to_all x1, waiting for transfers between devices, local(): lax.all_to_all(jnp.stack([rows_here] * lax.axis_size('tensor')), 'tensor'...  37 us
    unnamed x20, local copies, waits for them, and re-layouts  25.8 us
    broadcast_in_dim x2, other arithmetic, local(): return (weight_now[None], moment_now[None], jnp.stack(grads_out))  17 us
    dot_general x2, matrix products, local(): lax.dot_general(gathered, slope_grad, (((0,), (0,)), ((), ())), preferred...  14.7 us
  transfers between devices with their start and end apart: 7, of which 4 were waited for; matrix products, arithmetic and copies ran while one was open for 9% of the time, Pallas kernels for 0%

profile of v1, /device:TPU:0, one launch (start us, length us, event | category | flops | bytes accessed | tf_op | source)
XLA Modules:
  0.0 518.0 jit_solution(17351530630381749916)
XLA Ops:
  0.6 1.7 slice_bitcast_fusion
  2.4 2.5 stack.15
  4.9 5.2 %all-to-all-start = ((bf16[4,128,4096]{2,1,0:T(8,128)(2,1)}), bf16[4,128,4096]{2,1,0:T(8,128)(2,1)}, u32[]{:S(2)}, u32[]{:S(2)}) async-start(bf16[4,128,4096]{2,1,0:T(8,128)(2,1)} %stack.15), calls=%async_computation | async-start | bytes 8388608 | tf_op jit(solution)/shard_map/all_to_all | solution.py:67
  10.1 6.5 %copy.8 = bf16[1,4096,512]{1,2,0:T(8,128)(2,1)} copy(bf16[1,4096,512]{2,1,0:T(8,128)(2,1)} %param.5) | data formatting | bytes 8388608 | tf_op args[1]
  16.6 6.3 %copy.7 = bf16[1,4096,512]{1,2,0:T(8,128)(2,1)} copy(bf16[1,4096,512]{2,1,0:T(8,128)(2,1)} %param.4) | data formatting | bytes 8388608 | tf_op args[0]
  22.9 37.0 %all-to-all-done = bf16[4,128,4096]{2,1,0:T(8,128)(2,1)} async-done(((bf16[4,128,4096]{2,1,0:T(8,128)(2,1)}), bf16[4,128,4096]{2,1,0:T(8,128)(2,1)}, u32[]{:S(2)}, u32[]{:S(2)}) %all-to-all-start) | async-done | bytes 4194336 | tf_op jit(solution)/shard_map/all_to_all | solution.py:67
  59.9 0.0 copy-start.1
  59.9 0.0 copy-start.2
  59.9 0.0 copy-start.7
  59.9 5.9 %fusion.13 = f32[512,512]{1,0:T(8,128)S(1)} fusion(bf16[512,4096]{1,0:T(8,128)(2,1)} %bitcast.4, bf16[1,4096,512]{2,1,0:T(8,128)(2,1)} %param.4), kind=kOutput, calls=%fused_computation.23 | convolution fusion | flops 2147483648 | bytes 9437184 | tf_op jit(solution)/shard_map/dot_general | solution.py:69
  65.8 0.0 copy-done.1
  65.8 0.0 copy-done.2
  65.8 0.2 copy-done.7
  66.0 6.5 %fusion.1 = (bf16[4096,512]{0,1:T(8,128)(2,1)S(1)}, bf16[4096,512]{0,1:T(8,128)(2,1)S(1)}) fusion(bf16[1,4096,512]{1,2,0:T(8,128)(2,1)S(1)} %copy-done.2, bf16[512,4096]{1,0:T(8,128)(2,1)} %bitcast.4, f32[512,512]{1,0:T(8,128)S(1)} %fusion.13, bf16[2,512,512]{2,1,0:T(8,128)(2,1)S(1)} %copy-done.7, bf16[1,4096,512]{1,2,0:T(8,128)(2,1)S(1)} %copy-done.1), kind=kOutput, calls=%fused_computation.5 | convolution fusion | flops 2168979456 | bytes 22544384 | tf_op jit(solution)/shard_map/dot_general | solution.py:71
  72.5 0.0 copy-start.3
  72.6 1.7 collective-permute-start
  74.2 0.4 collective-permute-start.1
  74.7 0.5 stack.16
  75.2 225.2 %all_to_all.20 = bf16[4,128,4096]{2,1,0:T(8,128)(2,1)S(1)} all-to-all(bf16[4,128,4096]{2,1,0:T(8,128)(2,1)S(1)} %stack.16), channel_id=1, replica_groups=mesh['replica'=32,'tensor'=4] {'tensor'}, dimensions={0} | all-to-all | bytes 8388608 | tf_op jit(solution)/shard_map/all_to_all | solution.py:67
  300.3 0.0 collective-permute-done
  300.3 0.0 copy-start.5
  300.3 0.0 copy-done.3
  300.4 2.4 convolution_bitcast_fusion
  302.8 0.0 copy-done.5
  302.8 0.0 copy-start
  302.8 0.0 collective-permute-done.1
  302.8 8.2 %fusion.8 = bf16[4096,512]{0,1:T(8,128)(2,1)} fusion(bf16[4096,512]{0,1:T(8,128)(2,1)} %collective-permute-done.1, bf16[4096,512]{0,1:T(8,128)(2,1)S(1)} %get-tuple-element.11, bf16[512,4096]{1,0:T(8,128)(2,1)S(1)} %bitcast.63, f32[512,512]{1,0:T(8,128)S(1)} %convolution_bitcast_fusion, bf16[2,512,512]{2,1,0:T(8,128)(2,1)S(1)} %copy-done.7), kind=kOutput, calls=%fused_computation.13 | convolution fusion | flops 2168979456 | bytes 18350080 | tf_op jit(solution)/shard_map/dot_general | solution.py:71
  311.0 1.5 collective-permute-start.3
  312.5 0.0 copy-done
  312.5 4.5 convolution_convert_fusion.1
  317.1 4.8 all-to-all-start.2
  321.9 0.0 copy-start.4
  321.9 0.0 copy-start.6
  321.9 81.4 %collective-permute-done.3 = bf16[4096,512]{0,1:T(8,128)(2,1)} collective-permute-done((bf16[4096,512]{0,1:T(8,128)(2,1)}, bf16[4096,512]{0,1:T(8,128)(2,1)}, u32[]{:S(2)}, u32[]{:S(2)}) %collective-permute-start.3) | collective-permute-done | bytes 4194336 | tf_op jit(solution)/shard_map/ppermute | solution.py:29
  403.3 9.8 %fusion.11 = (bf16[1,4096,512]{1,2,0:T(8,128)(2,1)}, bf16[4096,512]{0,1:T(8,128)(2,1)}) fusion(bf16[4096,512]{0,1:T(8,128)(2,1)} %collective-permute-done.3, bf16[4096,512]{0,1:T(8,128)(2,1)} %fusion.8, bf16[4096,512]{0,1:T(8,128)(2,1)} %copy-done.5, bf16[4096,512]{0,1:T(8,128)(2,1)} %copy-done.3), kind=kLoop, calls=%fused_computation.21 | loop fusion | flops 29360128 | bytes 25165824 | tf_op jit(solution)/shard_map/broadcast_in_dim | solution.py:78
  413.1 1.5 collective-permute-start.2
  414.6 0.0 copy-done.4
  414.6 0.0 copy-done.6
  414.6 4.8 convolution_convert_fusion
  419.4 0.0 all-to-all-done.2
  419.4 4.9 all-to-all-start.3
  424.3 3.1 reduce_sum.24
  427.3 46.7 %all-to-all-done.3 = bf16[4,128,4096]{2,1,0:T(8,128)(2,1)} async-done(((bf16[4,128,4096]{2,1,0:T(8,128)(2,1)}), bf16[4,128,4096]{2,1,0:T(8,128)(2,1)}, u32[]{:S(2)}, u32[]{:S(2)}) %all-to-all-start.3) | async-done | bytes 4194336 | tf_op jit(solution)/shard_map/all_to_all | solution.py:18
  474.0 3.1 reduce_sum.25
  477.1 1.5 pad_maximum_fusion
  478.6 6.4 %copy.11 = bf16[1,4096,512]{2,1,0:T(8,128)(2,1)} copy(bf16[1,4096,512]{1,2,0:T(8,128)(2,1)} %get-tuple-element.6) | data formatting | bytes 8388608
  485.0 19.5 %collective-permute-done.2 = bf16[4096,512]{0,1:T(8,128)(2,1)} collective-permute-done((bf16[4096,512]{0,1:T(8,128)(2,1)}, bf16[4096,512]{0,1:T(8,128)(2,1)}, u32[]{:S(2)}, u32[]{:S(2)}) %collective-permute-start.2) | collective-permute-done | bytes 4194336 | tf_op jit(solution)/shard_map/ppermute | solution.py:29
  504.5 7.2 %fusion.10 = bf16[1,4096,512]{1,2,0:T(8,128)(2,1)} fusion(bf16[4096,512]{0,1:T(8,128)(2,1)} %collective-permute-done.2, bf16[4096,512]{0,1:T(8,128)(2,1)} %get-tuple-element.7), kind=kLoop, calls=%fused_computation.20 | loop fusion | flops 10485760 | bytes 12582912 | tf_op jit(solution)/shard_map/broadcast_in_dim | solution.py:78
  511.6 6.4 %copy.10 = bf16[1,4096,512]{2,1,0:T(8,128)(2,1)} copy(bf16[1,4096,512]{1,2,0:T(8,128)(2,1)} %fusion.10) | data formatting | bytes 8388608
Async XLA Ops:
  4.9 55.0 %all-to-all-start = ((bf16[4,128,4096]{2,1,0:T(8,128)(2,1)}), bf16[4,128,4096]{2,1,0:T(8,128)(2,1)}, u32[]{:S(2)}, u32[]{:S(2)}) async-start(bf16[4,128,4096]{2,1,0:T(8,128)(2,1)} %stack.15), calls=%async_computation | async-start | bytes 8388608 | tf_op jit(solution)/shard_map/all_to_all | solution.py:67
  59.9 5.9 %copy-start.1 = (bf16[1,4096,512]{1,2,0:T(8,128)(2,1)S(1)}, bf16[1,4096,512]{1,2,0:T(8,128)(2,1)}, u32[]{:S(2)}) copy-start(bf16[1,4096,512]{1,2,0:T(8,128)(2,1)} %copy.8) | copy-start | bytes 12582916
  59.9 5.9 %copy-start.2 = (bf16[1,4096,512]{1,2,0:T(8,128)(2,1)S(1)}, bf16[1,4096,512]{1,2,0:T(8,128)(2,1)}, u32[]{:S(2)}) copy-start(bf16[1,4096,512]{1,2,0:T(8,128)(2,1)} %copy.7) | copy-start | bytes 12582916
  59.9 6.1 %copy-start.7 = (bf16[2,512,512]{2,1,0:T(8,128)(2,1)S(1)}, bf16[2,512,512]{2,1,0:T(8,128)(2,1)}, u32[]{:S(2)}) copy-start(bf16[2,512,512]{2,1,0:T(8,128)(2,1)} %param.7) | copy-start | bytes 3145732
  72.5 227.8 %copy-start.3 = (bf16[4096,512]{0,1:T(8,128)(2,1)}, bf16[4096,512]{0,1:T(8,128)(2,1)S(1)}, u32[]{:S(2)}) copy-start(bf16[4096,512]{0,1:T(8,128)(2,1)S(1)} %get-tuple-element.10) | copy-start | bytes 12582916
  72.6 227.8 %collective-permute-start = (bf16[4096,512]{0,1:T(8,128)(2,1)S(1)}, bf16[4096,512]{0,1:T(8,128)(2,1)S(1)}, u32[]{:S(2)}, u32[]{:S(2)}) collective-permute-start(bf16[4096,512]{0,1:T(8,128)(2,1)S(1)} %get-tuple-element.10), channel_id=1, source_target_pairs={{0,4},{4,0},{8,12},{12,8},{16,20},{20,16},{24,28},{28,24},{32,36},... | collective-permute-start | bytes 12582920 | tf_op jit(solution)/shard_map/ppermute | solution.py:29
  74.2 228.6 %collective-permute-start.1 = (bf16[4096,512]{0,1:T(8,128)(2,1)S(1)}, bf16[4096,512]{0,1:T(8,128)(2,1)}, u32[]{:S(2)}, u32[]{:S(2)}) collective-permute-start(bf16[4096,512]{0,1:T(8,128)(2,1)S(1)} %get-tuple-element.11), channel_id=1, source_target_pairs={{0,4},{4,0},{8,12},{12,8},{16,20},{20,16},{24,28},{28,24},{32,36},... | collective-permute-start | bytes 12582920 | tf_op jit(solution)/shard_map/ppermute | solution.py:29
  300.3 2.5 copy-start.5
  302.8 9.7 %copy-start = (bf16[1,4096,512]{2,1,0:T(8,128)(2,1)S(1)}, bf16[1,4096,512]{2,1,0:T(8,128)(2,1)}, u32[]{:S(2)}) copy-start(bf16[1,4096,512]{2,1,0:T(8,128)(2,1)} %param.4) | copy-start | bytes 12582916
  311.0 92.2 %collective-permute-start.3 = (bf16[4096,512]{0,1:T(8,128)(2,1)}, bf16[4096,512]{0,1:T(8,128)(2,1)}, u32[]{:S(2)}, u32[]{:S(2)}) collective-permute-start(bf16[4096,512]{0,1:T(8,128)(2,1)} %fusion.8), channel_id=1, source_target_pairs={{0,8},{8,0},{4,12},{12,4},{16,24},{24,16},{20,28},{28,20},{32,40},... | collective-permute-start | bytes 12582920 | tf_op jit(solution)/shard_map/ppermute | solution.py:29
  317.1 102.4 %all-to-all-start.2 = ((bf16[4,128,4096]{2,1,0:T(8,128)(2,1)}), bf16[4,128,4096]{2,1,0:T(8,128)(2,1)}, u32[]{:S(2)}, u32[]{:S(2)}) async-start(bf16[4,128,4096]{2,1,0:T(8,128)(2,1)} %bitcast.60), calls=%async_computation.2 | async-start | bytes 8388608 | tf_op jit(solution)/shard_map/all_to_all | solution.py:18
  321.9 92.7 %copy-start.4 = (bf16[4096,512]{0,1:T(8,128)(2,1)S(1)}, bf16[4096,512]{0,1:T(8,128)(2,1)}, u32[]{:S(2)}) copy-start(bf16[4096,512]{0,1:T(8,128)(2,1)} %copy-done.3) | copy-start | bytes 12582916
  321.9 92.7 %copy-start.6 = (bf16[4096,512]{0,1:T(8,128)(2,1)S(1)}, bf16[4096,512]{0,1:T(8,128)(2,1)}, u32[]{:S(2)}) copy-start(bf16[4096,512]{0,1:T(8,128)(2,1)} %copy-done.5) | copy-start | bytes 12582916
  413.1 91.3 %collective-permute-start.2 = (bf16[4096,512]{0,1:T(8,128)(2,1)}, bf16[4096,512]{0,1:T(8,128)(2,1)}, u32[]{:S(2)}, u32[]{:S(2)}) collective-permute-start(bf16[4096,512]{0,1:T(8,128)(2,1)} %get-tuple-element.7), channel_id=1, source_target_pairs={{0,8},{8,0},{4,12},{12,4},{16,24},{24,16},{20,28},{28,20},{32,40},... | collective-permute-start | bytes 12582920 | tf_op jit(solution)/shard_map/ppermute | solution.py:29
  419.4 54.6 %all-to-all-start.3 = ((bf16[4,128,4096]{2,1,0:T(8,128)(2,1)}), bf16[4,128,4096]{2,1,0:T(8,128)(2,1)}, u32[]{:S(2)}, u32[]{:S(2)}) async-start(bf16[4,128,4096]{2,1,0:T(8,128)(2,1)} %bitcast.61), calls=%async_computation.3 | async-start | bytes 8388608 | tf_op jit(solution)/shard_map/all_to_all | solution.py:18
